TPU v7x, 32 devices: a whole 2x2x4 slice. The times are simulated.
32 devices in a mesh: slab: 2 (over x), gal: 4 (over y, core), qb: 4 (over z).
Axes of the slice: x: 2, y: 2, z: 4, core: 2. Of those that a mesh axis runs over, the one named last changes fastest.
Arguments:
- gallery: bfloat16 [16384, 768], P(('slab', 'gal')), parts along dimension 0, may hold values from -512 to 512
- querybank: bfloat16 [8, 2048, 768], P(('slab', 'qb'), 'gal'), parts along dimension 0, may hold values from -512 to 512
- test_queries: bfloat16 [8, 512, 768], P(('slab', 'qb'), 'gal'), parts along dimension 0, may hold values from -512 to 512
Outputs:
- logprob: float32 [4096, 8192], P(('slab', 'qb'), 'gal'), parts along dimension 0
- normalizer: float32 [16384], P(('slab', 'gal')), parts along dimension 0
There are 2 independent parts, one for each index of `slab`. A program takes and returns all parts, laid end to end along the dimension named above; each array names one. Nothing has to cross between parts.
All inputs are finite; a program needn't handle non-finite values.
Results may differ from a plain program's by a relative error of at most 0.00049.
Values may be sent and summed in bfloat16 or wider, within the bound.
No kernel may reach another device: no remote copies, remote signals or barrier semaphores. Data moves between devices by JAX's collectives and lax.ppermute only.
A program may use at most 64 MiB of HBM per device.

v0:
```python
import math
import jax
import jax.numpy as jnp
from jax import lax
from jax.sharding import PartitionSpec as P

sharpness = 20.0


def unit_rows(values):
    wide = values.astype(jnp.float32)
    scaled = wide * lax.rsqrt(jnp.sum(wide * wide, axis=-1, keepdims=True) + 1e-06)
    return scaled.astype(jnp.bfloat16)


def column_terms(bank_block, gallery_unit):
    scores = lax.dot_general(
        bank_block, gallery_unit, (((1,), (1,)), ((), ())), preferred_element_type=jnp.float32
    )
    return jnp.sum(jnp.exp(sharpness * (scores - 1.0)), axis=0)


def bank_columns(bank_block, gallery_unit):
    rows = bank_block.shape[0]
    height = math.gcd(rows, 512)

    def add_block(index, running):
        piece = lax.dynamic_slice_in_dim(bank_block, index * height, height, 0)
        return running + column_terms(piece, gallery_unit)

    initial = jnp.zeros((gallery_unit.shape[0],), jnp.float32)
    return lax.fori_loop(0, rows // height, add_block, initial)


def per_device(gallery, querybank, test_queries):
    gallery_unit = unit_rows(gallery)
    bank_local = unit_rows(querybank[0])
    test_local = unit_rows(test_queries[0])
    bank_all = lax.all_gather(bank_local, "gal", axis=0, tiled=True)
    column_part = bank_columns(bank_all, gallery_unit)
    test_all = lax.all_gather(test_local, "gal", axis=0, tiled=True)
    column_total = lax.psum(column_part, "qb")
    normalizer = sharpness + jnp.log(column_total)
    bank_count = querybank.shape[1] * lax.axis_size("gal") * lax.axis_size("qb")
    offset = 2.0 * sharpness - math.log(bank_count)
    scores = lax.dot_general(
        test_all, gallery_unit, (((1,), (1,)), ((), ())), preferred_element_type=jnp.float32
    )
    logits = sharpness * scores - normalizer[None, :] - offset
    row_part = jnp.sum(jnp.exp(logits), axis=1)
    row_total = lax.psum(row_part, "gal")
    logprob = logits - jnp.log(row_total)[:, None]
    return (logprob, normalizer)


def solution(mesh):
    placed = (
        P(("slab", "gal"), None),
        P(("slab", "qb"), "gal", None),
        P(("slab", "qb"), "gal", None),
    )
    return jax.shard_map(
        per_device,
        mesh=mesh,
        in_specs=placed,
        out_specs=(P(("slab", "qb"), "gal"), P(("slab", "gal"))),
        check_vma=False,
    )
```

profile of v0, /device:TPU:0, one launch (start us, length us, event | category | flops | bytes accessed | tf_op | source)
XLA Modules:
  0.0 94.0 jit_solution(4073056862240279345)
XLA Ops:
  7.2 0.0 copy-start.1
  7.2 0.0 copy-start
  7.2 0.0 all-gather.2.cloned.1.call-start
  7.2 1.5 %fusion.5 = f32[512]{0:T(512)S(1)} fusion(bf16[1,512,768]{2,1,0:T(8,128)(2,1)} %param.6), kind=kLoop, calls=%fused_computation.13 | loop fusion | flops 1179136 | bytes 788480 | tf_op jit(solution)/shard_map/reduce_sum | solution.py:12
  8.8 2.2 %fusion.6 = bf16[512,768]{1,0:T(8,128)(2,1)} fusion(bf16[1,512,768]{2,1,0:T(8,128)(2,1)} %param.6, f32[512]{0:T(512)S(1)} %add_rsqrt_fusion.1), kind=kLoop, calls=%fused_computation.14 | loop fusion | flops 1179648 | bytes 1574912 | tf_op jit(solution)/shard_map/convert_element_type | solution.py:13
  11.0 0.0 all-gather.2.cloned.1.call-update
  11.0 1.0 %fusion.7 = f32[128]{0:T(128)S(1)} fusion(bf16[1,128,768]{2,1,0:T(8,128)(2,1)} %param.7), kind=kLoop, calls=%fused_computation.17 | loop fusion | flops 294784 | bytes 197120 | tf_op jit(solution)/shard_map/reduce_sum | solution.py:12
  12.1 0.0 copy-done
  12.1 0.7 fusion.2
  12.8 0.0 copy-done.1
  12.8 0.1 fusion.8
  12.9 10.6 %all_gather.6 = bf16[512,768]{1,0:T(8,128)(2,1)} all-gather(bf16[128,768]{1,0:T(8,128)(2,1)S(1)} %fusion.8), channel_id=1, replica_groups=mesh['slab'=2,'gal'=4,'qb'=4] {'gal'}, dimensions={0}, use_global_device_ids=true | all-gather | bytes 983040 | tf_op jit(solution)/shard_map/all_gather | solution.py:41
  23.5 2.3 %fusion.3 = bf16[2048,768]{1,0:T(8,128)(2,1)} fusion(bf16[2048,768]{1,0:T(8,128)(2,1)S(1)} %copy-done, f32[2048]{0:T(1024)S(1)} %add_rsqrt_fusion), kind=kLoop, calls=%fused_computation.7 | loop fusion | flops 4718592 | bytes 6299648 | tf_op jit(solution)/shard_map/convert_element_type | solution.py:13
  25.8 16.6 %all-gather.2.cloned.1.call-done = bf16[2048,768]{1,0:T(8,128)(2,1)} async-done(((bf16[512,768]{1,0:T(8,128)(2,1)}), bf16[2048,768]{1,0:T(8,128)(2,1)}) %all-gather.2.cloned.1.call-update) | async-done | bytes 3145744 | tf_op jit(solution)/shard_map/all_gather | solution.py:39
  42.4 0.0 copy-start.2
  42.4 16.3 %while.16 = (s32[]{:T(128)}, f32[2048]{0:T(1024)S(1)}, bf16[2048,768]{1,0:T(8,128)(2,1)}, bf16[2048,768]{1,0:T(8,128)(2,1)}, s32[]{:T(128)}, /*index=5*/s32[]{:T(128)}, s32[]{:T(128)}, s32[]{:T(128)}) while((s32[]{:T(128)}, f32[2048]{0:T(1024)S(1)}, bf16[2048,768]{1,0:T(8,128)(2,1)}, bf16[2048,768]{1,0:T(8,128)(2,1)}, s32[]{:T(128)}, ...), condition=%wide.region_5.0_spmd.clone, body=%wide.region_3.0_spmd.clone.sunk | while | flops 1613760512 | bytes 3965081 | solution.py:32
  42.4 4.1 %exponential_reduce_fusion.3 = f32[2048]{0:T(1024)S(1)} fusion(bf16[2048,768]{1,0:T(8,128)(2,1)} %get-tuple-element.182, bf16[2048,768]{1,0:T(8,128)(2,1)} %get-tuple-element.181, s32[]{:T(128)S(6)} %select_n.12), kind=kOutput, calls=%fused_computation.clone.1 | convolution fusion | flops 1613756416 | bytes 3940356 | tf_op jit(solution)/shard_map/while/body/eval_jaxpr/dot_general | solution.py:17
  46.5 4.0 %exponential_reduce_fusion.3 = f32[2048]{0:T(1024)S(1)} fusion(bf16[2048,768]{1,0:T(8,128)(2,1)} %get-tuple-element.182, bf16[2048,768]{1,0:T(8,128)(2,1)} %get-tuple-element.181, s32[]{:T(128)S(6)} %select_n.12), kind=kOutput, calls=%fused_computation.clone.1 | convolution fusion | flops 1613756416 | bytes 3940356 | tf_op jit(solution)/shard_map/while/body/eval_jaxpr/dot_general | solution.py:17
  50.6 4.0 %exponential_reduce_fusion.3 = f32[2048]{0:T(1024)S(1)} fusion(bf16[2048,768]{1,0:T(8,128)(2,1)} %get-tuple-element.182, bf16[2048,768]{1,0:T(8,128)(2,1)} %get-tuple-element.181, s32[]{:T(128)S(6)} %select_n.12), kind=kOutput, calls=%fused_computation.clone.1 | convolution fusion | flops 1613756416 | bytes 3940356 | tf_op jit(solution)/shard_map/while/body/eval_jaxpr/dot_general | solution.py:17
  54.6 4.0 %exponential_reduce_fusion.3 = f32[2048]{0:T(1024)S(1)} fusion(bf16[2048,768]{1,0:T(8,128)(2,1)} %get-tuple-element.182, bf16[2048,768]{1,0:T(8,128)(2,1)} %get-tuple-element.181, s32[]{:T(128)S(6)} %select_n.12), kind=kOutput, calls=%fused_computation.clone.1 | convolution fusion | flops 1613756416 | bytes 3940356 | tf_op jit(solution)/shard_map/while/body/eval_jaxpr/dot_general | solution.py:17
  58.7 11.8 %psum.14 = f32[2048]{0:T(1024)S(1)} all-reduce(f32[2048]{0:T(1024)S(1)} %get-tuple-element.112), channel_id=1, replica_groups=mesh['slab'=2,'gal'=4,'qb'=4] {'qb'}, use_global_device_ids=true, to_apply=%region_6.0 | all-reduce | flops 2048 | bytes 16384 | tf_op jit(solution)/shard_map/psum | solution.py:42
  70.5 0.0 copy-done.2
  70.5 0.0 copy-start.3
  70.6 5.9 %exponential_reduce_fusion.1 = (f32[512]{0:T(512)S(1)}, f32[512,2048]{1,0:T(8,128)}) fusion(f32[2048]{0:T(1024)S(1)} %log_add_fusion, bf16[512,768]{1,0:T(8,128)(2,1)S(1)} %copy-done.2, bf16[2048,768]{1,0:T(8,128)(2,1)} %get-tuple-element.188), kind=kOutput, calls=%fused_computation.8 | convolution fusion | flops 1614806528 | bytes 8136704 | tf_op jit(solution)/shard_map/dot_general | solution.py:46
  76.5 5.9 %psum.15 = f32[512]{0:T(512)S(1)} all-reduce(f32[512]{0:T(512)S(1)} %get-tuple-element.136), channel_id=1, replica_groups=mesh['slab'=2,'gal'=4,'qb'=4] {'gal'}, use_global_device_ids=true, to_apply=%region_8.0 | all-reduce | flops 512 | bytes 4096 | tf_op jit(solution)/shard_map/psum | solution.py:51
  82.4 0.0 copy-done.3
  82.4 4.8 %fusion.4 = f32[512,2048]{1,0:T(8,128)} fusion(f32[512,2048]{1,0:T(8,128)} %get-tuple-element.137, f32[512]{0:T(512)S(1)} %log.7, f32[2048]{0:T(1024)S(1)} %log_add_fusion), kind=kLoop, calls=%fused_computation.10 | loop fusion | flops 4194304 | bytes 8398848 | tf_op jit(solution)/shard_map/sub | solution.py:52
  (10 shorter events, 0.1 us)
Async XLA Ops:
  7.2 5.6 %copy-start.1 = (bf16[1,128,768]{2,1,0:T(8,128)(2,1)S(1)}, bf16[1,128,768]{2,1,0:T(8,128)(2,1)}, u32[]{:S(2)}) copy-start(bf16[1,128,768]{2,1,0:T(8,128)(2,1)} %param.7) | copy-start | bytes 589828
  7.2 4.9 %copy-start = (bf16[2048,768]{1,0:T(8,128)(2,1)S(1)}, bf16[2048,768]{1,0:T(8,128)(2,1)}, u32[]{:S(2)}) copy-start(bf16[2048,768]{1,0:T(8,128)(2,1)} %param.5) | copy-start | bytes 9437188
  7.2 35.2 %all-gather.2.cloned.1.call-start = ((), (), s32[]{:S(2)}) async-start(), calls=%async_computation | async-start | bytes 3932160 | tf_op jit(solution)/shard_map/all_gather | solution.py:39
  42.4 28.2 %copy-start.2 = (bf16[512,768]{1,0:T(8,128)(2,1)S(1)}, bf16[512,768]{1,0:T(8,128)(2,1)}, u32[]{:S(2)}) copy-start(bf16[512,768]{1,0:T(8,128)(2,1)} %all_gather.6) | copy-start | bytes 2359300
  70.5 11.9 %copy-start.3 = (f32[2048]{0:T(1024)}, f32[2048]{0:T(1024)S(1)}, u32[]{:S(2)}) copy-start(f32[2048]{0:T(1024)S(1)} %log_add_fusion) | copy-start | bytes 24580
Sparse Core Ops, SparseCore 0:
  11.1 31.2 all-gather.1
where the time goes:
time: 94.4 us; the launch traced here: 94 us
  blocking collectives  28.3 us (30%)
  matrix products  22.1 us (23%)
  waiting for transfers between devices  16.6 us (18%)
  between operations  14.1 us (15%)
  other arithmetic  12.7 us (13%)
    all_gather x1, waiting for transfers between devices, per_device(): bank_all = lax.all_gather(bank_local, 'gal', axis=0, tiled=True)  16.6 us
    dot_general x4, matrix products, column_terms(): lax.dot_general(bank_block, gallery_unit, (((1,), (1,)), ((), ())), prefe...  16.1 us
    psum x1, blocking collectives, per_device(): column_total = lax.psum(column_part, 'qb')  11.8 us
    all_gather x1, blocking collectives, per_device(): test_all = lax.all_gather(test_local, 'gal', axis=0, tiled=True)  10.6 us
    dot_general x1, matrix products, per_device(): lax.dot_general(test_all, gallery_unit, (((1,), (1,)), ((), ())), preferr...  5.95 us
    psum x1, blocking collectives, per_device(): row_total = lax.psum(row_part, 'gal')  5.9 us
    sub x1, other arithmetic, per_device(): logprob = logits - jnp.log(row_total)[:, None]  4.79 us
    convert_element_type x3, other arithmetic, unit_rows(): return scaled.astype(jnp.bfloat16)  4.59 us
  transfers between devices with their start and end apart: 1, of which 1 were waited for; matrix products, arithmetic and copies ran while one was open for 4% of the time, Pallas kernels for 0%

commit v1 on v0

--- a/solution.py
+++ b/solution.py
@@ -5,6 +5,28 @@
 from jax.sharding import PartitionSpec as P
 
 sharpness = 20.0
+
+
+def laid_out(parts, dim):
+    parts = jnp.moveaxis(parts, 0, dim)
+    dims = parts.shape
+    return parts.reshape(*dims[:dim], dims[dim] * dims[dim + 1], *dims[dim + 2 :])
+
+
+def collected_by_bits(array, axis):
+    devices = lax.axis_size(axis)
+    parts = array[None]
+    for level in range(devices.bit_length() - 1):
+        apart = 1 << level
+        received = lax.ppermute(parts, axis, [(i, i ^ apart) for i in range(devices)])
+        both = jnp.stack([parts, received])
+        upper = lax.axis_index(axis) >> level & 1
+        parts = jnp.where(upper == 0, both, both[::-1]).reshape(-1, *array.shape)
+    return parts
+
+
+def doubled_up(value, axis, dim):
+    return laid_out(collected_by_bits(value, axis), dim)
 
 
 def unit_rows(values):
@@ -38,7 +60,7 @@
     test_local = unit_rows(test_queries[0])
     bank_all = lax.all_gather(bank_local, "gal", axis=0, tiled=True)
     column_part = bank_columns(bank_all, gallery_unit)
-    test_all = lax.all_gather(test_local, "gal", axis=0, tiled=True)
+    test_all = doubled_up(test_local, "gal", 0)
     column_total = lax.psum(column_part, "qb")
     normalizer = sharpness + jnp.log(column_total)
     bank_count = querybank.shape[1] * lax.axis_size("gal") * lax.axis_size("qb")

time: 94.4 us -> 98.5 us (1.043)
  blocking collectives: 28.3 us -> 18 us
  waiting for transfers between devices: 16.6 us -> 25.7 us
  starting transfers between devices: 0.04 us -> 3.2 us
  other arithmetic: 12.7 us -> 15 us
    ppermute x0 -> x2, waiting for transfers between devices: none -> 12.5 us  [collected_by_bits(): lax.ppermute(parts, axis, [(i, i ^ apart) for i in range(devices)])]
    all_gather x1 -> x0, blocking collectives: 10.6 us -> none  [per_device(): test_all = lax.all_gather(test_local, 'gal', axis=0, tiled=True)]
    all_gather x1, waiting for transfers between devices: 16.6 us -> 13.1 us  [per_device(): bank_all = lax.all_gather(bank_local, 'gal', axis=0, tiled=True)]
    ppermute x0 -> x2, starting transfers between devices: none -> 3.16 us  [collected_by_bits(): lax.ppermute(parts, axis, [(i, i ^ apart) for i in range(devices)])]
    convert_element_type x3 -> x4, other arithmetic: 4.59 us -> 6.54 us  [unit_rows(): return scaled.astype(jnp.bfloat16)]
  transfers between devices with their start and end apart: 1 -> 3, of which waited for: 1 -> 2; matrix products, arithmetic and copies ran while one was open for 4% -> 7% of each run, Pallas kernels for 0% -> 0%
where the time goes in v1:
time: 98.5 us; the launch traced here: 98.1 us
  waiting for transfers between devices  25.7 us (26%)
  matrix products  22 us (22%)
  blocking collectives  18 us (18%)
  other arithmetic  15 us (15%)
  between operations  14.1 us (14%)
  starting transfers between devices  3.2 us (3%)
    dot_general x4, matrix products, column_terms(): lax.dot_general(bank_block, gallery_unit, (((1,), (1,)), ((), ())), prefe...  16.1 us
    all_gather x1, waiting for transfers between devices, per_device(): bank_all = lax.all_gather(bank_local, 'gal', axis=0, tiled=True)  13.1 us
    ppermute x2, waiting for transfers between devices, collected_by_bits(): lax.ppermute(parts, axis, [(i, i ^ apart) for i in range(devices)])  12.5 us
    psum x1, blocking collectives, per_device(): column_total = lax.psum(column_part, 'qb')  12.3 us
    convert_element_type x4, other arithmetic, unit_rows(): return scaled.astype(jnp.bfloat16)  6.54 us
    dot_general x1, matrix products, per_device(): lax.dot_general(test_all, gallery_unit, (((1,), (1,)), ((), ())), preferr...  5.95 us
    psum x1, blocking collectives, per_device(): row_total = lax.psum(row_part, 'gal')  5.63 us
    sub x1, other arithmetic, per_device(): logprob = logits - jnp.log(row_total)[:, None]  4.79 us
  transfers between devices with their start and end apart: 3, of which 2 were waited for; matrix products, arithmetic and copies ran while one was open for 7% of the time, Pallas kernels for 0%

profile of v1, /device:TPU:0, one launch (start us, length us, event | category | flops | bytes accessed | tf_op | source)
XLA Modules:
  0.0 98.1 jit_solution(3659482057743307043)
XLA Ops:
  7.2 0.0 copy-start
  7.2 0.0 all-gather.2.cloned.1.call-start
  7.2 1.5 %fusion.5 = f32[512]{0:T(512)S(1)} fusion(bf16[1,512,768]{2,1,0:T(8,128)(2,1)} %param.6), kind=kLoop, calls=%fused_computation.13 | loop fusion | flops 1179136 | bytes 788480 | tf_op jit(solution)/shard_map/reduce_sum | solution.py:34
  8.7 2.2 %fusion.6 = bf16[512,768]{1,0:T(8,128)(2,1)} fusion(bf16[1,512,768]{2,1,0:T(8,128)(2,1)} %param.6, f32[512]{0:T(512)S(1)} %add_rsqrt_fusion.1), kind=kLoop, calls=%fused_computation.14 | loop fusion | flops 1179648 | bytes 1574912 | tf_op jit(solution)/shard_map/convert_element_type | solution.py:35
  11.0 0.0 all-gather.2.cloned.1.call-update
  11.0 1.0 %fusion.9 = f32[128]{0:T(128)S(1)} fusion(bf16[1,128,768]{2,1,0:T(8,128)(2,1)} %param.7), kind=kLoop, calls=%fused_computation.23 | loop fusion | flops 294784 | bytes 197120 | tf_op jit(solution)/shard_map/reduce_sum | solution.py:34
  12.0 1.0 %fusion.10 = bf16[1,128,768]{2,1,0:T(8,128)(2,1)S(1)} fusion(bf16[1,128,768]{2,1,0:T(8,128)(2,1)} %param.7, f32[128]{0:T(128)S(1)} %add_rsqrt_fusion.2), kind=kLoop, calls=%fused_computation.24 | loop fusion | flops 294912 | bytes 393728 | tf_op jit(solution)/shard_map/convert_element_type | solution.py:35
  13.1 0.6 collective-permute-start
  13.6 1.0 %fusion.8 = bf16[1,1,128,768]{3,2,1,0:T(8,128)(2,1)S(1)} fusion(bf16[1,128,768]{2,1,0:T(8,128)(2,1)} %param.7, f32[128]{0:T(128)S(1)} %add_rsqrt_fusion.2), kind=kLoop, calls=%fused_computation.22 | loop fusion | flops 294912 | bytes 393728 | tf_op jit(solution)/shard_map/convert_element_type | solution.py:35
  14.7 0.0 copy-done
  14.7 0.7 fusion.2
  15.4 0.0 collective-permute-done
  15.4 0.1 fusion.12
  15.5 2.6 %collective-permute-start.1 = (bf16[2,128,768]{2,1,0:T(8,128)(2,1)S(1)}, bf16[2,128,768]{2,1,0:T(8,128)(2,1)S(1)}, u32[]{:S(2)}, u32[]{:S(2)}) collective-permute-start(bf16[2,128,768]{2,1,0:T(8,128)(2,1)S(1)} %get-tuple-element.137), channel_id=1, source_target_pairs={{0,8},{4,12},{8,0},{12,4},{1,9},{5,13},{9,1},{13,5},{2,10},{6,14},... | collective-permute-start | bytes 1179656 | tf_op jit(solution)/shard_map/ppermute | solution.py:21
  18.1 2.3 %fusion.3 = bf16[2048,768]{1,0:T(8,128)(2,1)} fusion(bf16[2048,768]{1,0:T(8,128)(2,1)S(1)} %copy-done, f32[2048]{0:T(1024)S(1)} %add_rsqrt_fusion), kind=kLoop, calls=%fused_computation.7 | loop fusion | flops 4718592 | bytes 6299648 | tf_op jit(solution)/shard_map/convert_element_type | solution.py:35
  20.4 12.5 %collective-permute-done.1 = bf16[2,128,768]{2,1,0:T(8,128)(2,1)S(1)} collective-permute-done((bf16[2,128,768]{2,1,0:T(8,128)(2,1)S(1)}, bf16[2,128,768]{2,1,0:T(8,128)(2,1)S(1)}, u32[]{:S(2)}, u32[]{:S(2)}) %collective-permute-start.1) | collective-permute-done | bytes 393248 | tf_op jit(solution)/shard_map/ppermute | solution.py:21
  32.9 0.1 pad_maximum_fusion
  33.0 0.1 reverse_select_fusion
  33.2 13.1 %all-gather.2.cloned.1.call-done = bf16[2048,768]{1,0:T(8,128)(2,1)} async-done(((bf16[512,768]{1,0:T(8,128)(2,1)}), bf16[2048,768]{1,0:T(8,128)(2,1)}) %all-gather.2.cloned.1.call-update) | async-done | bytes 3145744 | tf_op jit(solution)/shard_map/all_gather | solution.py:61
  46.3 16.2 %while.16 = (s32[]{:T(128)}, f32[2048]{0:T(1024)S(1)}, bf16[2048,768]{1,0:T(8,128)(2,1)}, bf16[2048,768]{1,0:T(8,128)(2,1)}, s32[]{:T(128)}, /*index=5*/s32[]{:T(128)}, s32[]{:T(128)}, s32[]{:T(128)}) while((s32[]{:T(128)}, f32[2048]{0:T(1024)S(1)}, bf16[2048,768]{1,0:T(8,128)(2,1)}, bf16[2048,768]{1,0:T(8,128)(2,1)}, s32[]{:T(128)}, ...), condition=%wide.region_5.0_spmd.clone, body=%wide.region_3.0_spmd.clone.sunk | while | flops 1613760512 | bytes 3965081 | solution.py:54
  46.3 4.0 %exponential_reduce_fusion.3 = f32[2048]{0:T(1024)S(1)} fusion(bf16[2048,768]{1,0:T(8,128)(2,1)} %get-tuple-element.184, bf16[2048,768]{1,0:T(8,128)(2,1)} %get-tuple-element.183, s32[]{:T(128)S(6)} %select_n.44), kind=kOutput, calls=%fused_computation.clone.1 | convolution fusion | flops 1613756416 | bytes 3940356 | tf_op jit(solution)/shard_map/while/body/eval_jaxpr/dot_general | solution.py:39
  50.4 4.0 %exponential_reduce_fusion.3 = f32[2048]{0:T(1024)S(1)} fusion(bf16[2048,768]{1,0:T(8,128)(2,1)} %get-tuple-element.184, bf16[2048,768]{1,0:T(8,128)(2,1)} %get-tuple-element.183, s32[]{:T(128)S(6)} %select_n.44), kind=kOutput, calls=%fused_computation.clone.1 | convolution fusion | flops 1613756416 | bytes 3940356 | tf_op jit(solution)/shard_map/while/body/eval_jaxpr/dot_general | solution.py:39
  54.4 4.0 %exponential_reduce_fusion.3 = f32[2048]{0:T(1024)S(1)} fusion(bf16[2048,768]{1,0:T(8,128)(2,1)} %get-tuple-element.184, bf16[2048,768]{1,0:T(8,128)(2,1)} %get-tuple-element.183, s32[]{:T(128)S(6)} %select_n.44), kind=kOutput, calls=%fused_computation.clone.1 | convolution fusion | flops 1613756416 | bytes 3940356 | tf_op jit(solution)/shard_map/while/body/eval_jaxpr/dot_general | solution.py:39
  58.5 4.0 %exponential_reduce_fusion.3 = f32[2048]{0:T(1024)S(1)} fusion(bf16[2048,768]{1,0:T(8,128)(2,1)} %get-tuple-element.184, bf16[2048,768]{1,0:T(8,128)(2,1)} %get-tuple-element.183, s32[]{:T(128)S(6)} %select_n.44), kind=kOutput, calls=%fused_computation.clone.1 | convolution fusion | flops 1613756416 | bytes 3940356 | tf_op jit(solution)/shard_map/while/body/eval_jaxpr/dot_general | solution.py:39
  62.5 12.3 %psum.14 = f32[2048]{0:T(1024)S(1)} all-reduce(f32[2048]{0:T(1024)S(1)} %get-tuple-element.112), channel_id=1, replica_groups=mesh['slab'=2,'gal'=4,'qb'=4] {'qb'}, use_global_device_ids=true, to_apply=%region_6.7 | all-reduce | flops 2048 | bytes 16384 | tf_op jit(solution)/shard_map/psum | solution.py:64
  74.9 0.0 copy-start.1
  74.9 6.0 %exponential_reduce_fusion.1 = (f32[512]{0:T(512)S(1)}, f32[512,2048]{1,0:T(8,128)}) fusion(f32[2048]{0:T(1024)S(1)} %log_add_fusion, bf16[512,768]{1,0:T(8,128)(2,1)S(1)} %bitcast.22, bf16[2048,768]{1,0:T(8,128)(2,1)} %get-tuple-element.190), kind=kOutput, calls=%fused_computation.8 | convolution fusion | flops 1614806528 | bytes 8136704 | tf_op jit(solution)/shard_map/dot_general | solution.py:68
  80.9 5.6 %psum.15 = f32[512]{0:T(512)S(1)} all-reduce(f32[512]{0:T(512)S(1)} %get-tuple-element.138), channel_id=1, replica_groups=mesh['slab'=2,'gal'=4,'qb'=4] {'gal'}, use_global_device_ids=true, to_apply=%region_8.9 | all-reduce | flops 512 | bytes 4096 | tf_op jit(solution)/shard_map/psum | solution.py:73
  86.5 0.0 copy-done.1
  86.5 4.8 %fusion.4 = f32[512,2048]{1,0:T(8,128)} fusion(f32[512,2048]{1,0:T(8,128)} %get-tuple-element.139, f32[512]{0:T(512)S(1)} %log.7, f32[2048]{0:T(1024)S(1)} %log_add_fusion), kind=kLoop, calls=%fused_computation.10 | loop fusion | flops 4194304 | bytes 8398848 | tf_op jit(solution)/shard_map/sub | solution.py:74
  (11 shorter events, 0.1 us)
Async XLA Ops:
  7.2 7.5 %copy-start = (bf16[2048,768]{1,0:T(8,128)(2,1)S(1)}, bf16[2048,768]{1,0:T(8,128)(2,1)}, u32[]{:S(2)}) copy-start(bf16[2048,768]{1,0:T(8,128)(2,1)} %param.5) | copy-start | bytes 9437188
  7.2 39.1 %all-gather.2.cloned.1.call-start = ((), (), s32[]{:S(2)}) async-start(), calls=%async_computation | async-start | bytes 3932160 | tf_op jit(solution)/shard_map/all_gather | solution.py:61
  13.1 2.3 %collective-permute-start = (bf16[1,128,768]{2,1,0:T(8,128)(2,1)S(1)}, bf16[1,128,768]{2,1,0:T(8,128)(2,1)S(1)}, u32[]{:S(2)}, u32[]{:S(2)}) collective-permute-start(bf16[1,128,768]{2,1,0:T(8,128)(2,1)S(1)} %fusion.10), channel_id=1, source_target_pairs={{0,4},{4,0},{8,12},{12,8},{1,5},{5,1},{9,13},{13,9},{2,6},{6,2},{1... | collective-permute-start | bytes 589832 | tf_op jit(solution)/shard_map/ppermute | solution.py:21
  15.5 17.4 %collective-permute-start.1 = (bf16[2,128,768]{2,1,0:T(8,128)(2,1)S(1)}, bf16[2,128,768]{2,1,0:T(8,128)(2,1)S(1)}, u32[]{:S(2)}, u32[]{:S(2)}) collective-permute-start(bf16[2,128,768]{2,1,0:T(8,128)(2,1)S(1)} %get-tuple-element.137), channel_id=1, source_target_pairs={{0,8},{4,12},{8,0},{12,4},{1,9},{5,13},{9,1},{13,5},{2,10},{6,14},... | collective-permute-start | bytes 1179656 | tf_op jit(solution)/shard_map/ppermute | solution.py:21
  74.9 11.6 %copy-start.1 = (f32[2048]{0:T(1024)}, f32[2048]{0:T(1024)S(1)}, u32[]{:S(2)}) copy-start(f32[2048]{0:T(1024)S(1)} %log_add_fusion) | copy-start | bytes 24580
Sparse Core Ops, SparseCore 0:
  11.1 35.1 all-gather.1
